TPU v7x, 32 devices: a whole 2x2x4 slice. The times are simulated.
32 devices in a mesh: rep: 8 (over z, y), shard: 4 (over x, core).
Axes of the slice: x: 2, y: 2, z: 4, core: 2. Of those that a mesh axis runs over, the one named last changes fastest.
Arguments:
- tokens: bfloat16 [4096, 1024], P(('rep', 'shard')), may hold values from -6 to 6
- cotangent: bfloat16 [4096, 1024], P(('rep', 'shard')), may hold values from -6 to 6
- doc_ids: int32 [4096], P(('rep', 'shard')), may hold values from -1 to 15, as said below
- w_query: bfloat16 [1024, 1024], P('shard'), may hold values from -0.1875 to 0.1875
- w_key: bfloat16 [1024, 512], P('shard'), may hold values from -0.1875 to 0.1875
- w_value: bfloat16 [1024, 512], P('shard'), may hold values from -0.1875 to 0.1875
- w_out: bfloat16 [1024, 1024], P('shard'), may hold values from -0.5 to 0.5
- w_gate: bfloat16 [1024, 4608], P('shard'), may hold values from -0.1875 to 0.1875
- w_up: bfloat16 [1024, 4608], P('shard'), may hold values from -0.1875 to 0.1875
- w_down: bfloat16 [4608, 1024], P('shard'), may hold values from -0.09375 to 0.09375
- gain_attn: bfloat16 [1024], P('shard'), may hold values from 0.5 to 1.5
- gain_ffn: bfloat16 [1024], P('shard'), may hold values from 0.5 to 1.5
- gain_query: bfloat16 [64], P('shard'), may hold values from 0.5 to 1.5
- gain_key: bfloat16 [64], P('shard'), may hold values from 0.5 to 1.5
Outputs:
- block_out: bfloat16 [4096, 1024], P(('rep', 'shard'))
- grad_tokens: float32 [4096, 1024], P(('rep', 'shard'))
- grad_w_query: float32 [1024, 1024], P('shard')
- grad_w_key: float32 [1024, 512], P('shard')
- grad_w_value: float32 [1024, 512], P('shard')
- grad_w_out: float32 [1024, 1024], P('shard')
- grad_w_gate: float32 [1024, 4608], P('shard')
- grad_w_up: float32 [1024, 4608], P('shard')
- grad_w_down: float32 [4608, 1024], P('shard')
- grad_gain_attn: float32 [1024], P('shard')
- grad_gain_ffn: float32 [1024], P('shard')
- grad_gain_query: float32 [64], P('shard')
- grad_gain_key: float32 [64], P('shard')
Inputs may be any that keep to these rules, and one draw needn't show every extreme that they name: `doc_ids`: each device's 128 slots hold its sequences one after another, numbered from 0 upward without gaps, followed by its empty slots marked -1; at least one device has no empty slot and holds 16 sequences.
All inputs are finite; a program needn't handle non-finite values.
Results may differ from a plain program's by a relative error of at most 0.02.
Values may be sent and summed in bfloat16 or wider, within the bound.
A program may use at most 192 MiB of HBM per device.

v0:
```python
import math
import jax
import jax.numpy as jnp
from jax import lax
from jax.sharding import PartitionSpec as P

QH = 16
KVH = 8
HEAD_DIM = 64
NORM_EPSILON = 1e-05
ROPE_BASE = 1000000.0


def matmul(left, right):
    return jnp.dot(left, right, preferred_element_type=jnp.float32)


def norm_rows(values, gain_vec):
    inv_rms = lax.rsqrt(jnp.mean(values * values, axis=-1, keepdims=True) + NORM_EPSILON)
    normed = values * inv_rms
    return (normed * gain_vec.astype(jnp.float32), normed, inv_rms)


def norm_back(grad_out, normed, inv_rms, gain_vec):
    scaled = grad_out * gain_vec.astype(jnp.float32)
    grad_in = inv_rms * (scaled - normed * jnp.mean(scaled * normed, axis=-1, keepdims=True))
    lead_axes = tuple(range(grad_out.ndim - 1))
    return (grad_in, jnp.sum(grad_out * normed, axis=lead_axes))


def doc_tables(doc_rows):
    block_len = doc_rows.shape[-1]
    row_index = jnp.arange(block_len)[:, None]
    col_index = jnp.arange(block_len)[None, :]
    same_doc = doc_rows[:, :, None] == doc_rows[:, None, :]
    allowed = same_doc & (row_index >= col_index)[None]
    earlier = same_doc & (row_index > col_index)[None]
    positions = jnp.sum(earlier.astype(jnp.int32), axis=2)
    return (allowed, positions)


def rope_tables(positions, head_dim):
    half_dim = head_dim // 2
    inv_freq = jnp.exp(
        jnp.arange(half_dim).astype(jnp.float32) * (-2.0 * math.log(ROPE_BASE) / head_dim)
    )
    angles = positions.astype(jnp.float32)[:, :, None, None] * inv_freq
    return (jnp.cos(angles), jnp.sin(angles))


def rotate(values, cos_tab, sin_tab):
    half_dim = values.shape[-1] // 2
    part_one = values[..., :half_dim]
    part_two = values[..., half_dim:]
    return jnp.concatenate(
        [part_one * cos_tab - part_two * sin_tab, part_two * cos_tab + part_one * sin_tab], axis=-1
    )


def rotate_back(values, cos_tab, sin_tab):
    half_dim = values.shape[-1] // 2
    part_one = values[..., :half_dim]
    part_two = values[..., half_dim:]
    return jnp.concatenate(
        [part_one * cos_tab + part_two * sin_tab, part_two * cos_tab - part_one * sin_tab], axis=-1
    )


def attn_probs_of(query_bf, key_bf, key_mask, log_total, score_scale):
    scores = (
        jnp.einsum("gqkrd,gskd->gkrqs", query_bf, key_bf, preferred_element_type=jnp.float32)
        * score_scale
    )
    if log_total is None:
        log_total = jnp.log(
            jnp.sum(jnp.where(key_mask, jnp.exp(scores), 0.0), axis=-1, keepdims=True)
        )
    return (jnp.where(key_mask, jnp.exp(scores - log_total), 0.0), log_total)


def local(
    tokens,
    cotangent,
    doc_ids,
    w_query,
    w_key,
    w_value,
    w_out,
    w_gate,
    w_up,
    w_down,
    gain_attn,
    gain_ffn,
    gain_query,
    gain_key,
):
    tok_rows = tokens.shape[0]
    head_share = QH // KVH
    score_scale = 1.0 / math.sqrt(HEAD_DIM)
    doc_rows = doc_ids[None, :]
    allowed, positions = doc_tables(doc_rows)
    key_mask = allowed[:, None, None]
    cos_tab, sin_tab = rope_tables(positions, HEAD_DIM)
    attn_set = (
        lax.all_gather(w_query, "shard", axis=0, tiled=True),
        lax.all_gather(w_key, "shard", axis=0, tiled=True),
        lax.all_gather(w_value, "shard", axis=0, tiled=True),
        lax.all_gather(w_out, "shard", axis=0, tiled=True),
        lax.all_gather(gain_attn, "shard", axis=0, tiled=True),
        lax.all_gather(gain_query, "shard", axis=0, tiled=True),
        lax.all_gather(gain_key, "shard", axis=0, tiled=True),
    )
    full_query, full_key, full_value, full_out, full_gattn, full_gquery, full_gkey = attn_set
    resid_in = tokens.astype(jnp.float32)
    normed_in, unit_in, rms_in = norm_rows(resid_in, full_gattn)
    normed_bf = normed_in.astype(jnp.bfloat16)
    query_raw = matmul(normed_bf, full_query).reshape(1, tok_rows, QH, HEAD_DIM)
    key_raw = matmul(normed_bf, full_key).reshape(1, tok_rows, KVH, HEAD_DIM)
    value_bf = (
        matmul(normed_bf, full_value).astype(jnp.bfloat16).reshape(1, tok_rows, KVH, HEAD_DIM)
    )
    query_normed, query_unit, query_rms = norm_rows(query_raw, full_gquery)
    key_normed, key_unit, key_rms = norm_rows(key_raw, full_gkey)
    query_bf = (
        rotate(query_normed, cos_tab, sin_tab)
        .astype(jnp.bfloat16)
        .reshape(1, tok_rows, KVH, head_share, HEAD_DIM)
    )
    key_bf = rotate(key_normed, cos_tab, sin_tab).astype(jnp.bfloat16)
    attn_probs, log_total = attn_probs_of(query_bf, key_bf, key_mask, None, score_scale)
    mixed_bf = (
        jnp.einsum(
            "gkrqs,gskd->gqkrd",
            attn_probs.astype(jnp.bfloat16),
            value_bf,
            preferred_element_type=jnp.float32,
        )
        .astype(jnp.bfloat16)
        .reshape(tok_rows, QH * HEAD_DIM)
    )
    resid_mid = resid_in + matmul(mixed_bf, full_out)
    ffn_set = (
        lax.all_gather(w_gate, "shard", axis=0, tiled=True),
        lax.all_gather(w_up, "shard", axis=0, tiled=True),
        lax.all_gather(w_down, "shard", axis=0, tiled=True),
        lax.all_gather(gain_ffn, "shard", axis=0, tiled=True),
    )
    full_gate, full_up, full_down, full_gffn = ffn_set
    normed_mid, unit_mid, rms_mid = norm_rows(resid_mid, full_gffn)
    hidden_in = normed_mid.astype(jnp.bfloat16)
    gate_proj = matmul(hidden_in, full_gate)
    up_proj = matmul(hidden_in, full_up)
    gate_sig = jax.nn.sigmoid(gate_proj)
    gate_act = gate_proj * gate_sig
    hidden_bf = (gate_act * up_proj).astype(jnp.bfloat16)
    block_out = (resid_mid + matmul(hidden_bf, full_down)).astype(jnp.bfloat16)
    back_gate, back_up, back_down, back_gffn = (
        lax.all_gather(w_gate, "shard", axis=0, tiled=True),
        lax.all_gather(w_up, "shard", axis=0, tiled=True),
        lax.all_gather(w_down, "shard", axis=0, tiled=True),
        lax.all_gather(gain_ffn, "shard", axis=0, tiled=True),
    )
    live_rows = (doc_ids >= 0).astype(jnp.float32)[:, None]
    grad_y = cotangent.astype(jnp.float32) * live_rows
    grad_y_bf = grad_y.astype(jnp.bfloat16)
    part_down = matmul(hidden_bf.T, grad_y_bf)
    grad_down = lax.psum_scatter(
        part_down.astype(jnp.bfloat16), "shard", scatter_dimension=0, tiled=True
    ).astype(jnp.float32)
    grad_down = lax.psum(grad_down.astype(jnp.bfloat16), "rep").astype(jnp.float32)
    grad_hidden = matmul(grad_y_bf, back_down.T)
    grad_gate_bf = (grad_hidden * up_proj * gate_sig * (1.0 + gate_proj * (1.0 - gate_sig))).astype(
        jnp.bfloat16
    )
    grad_up_bf = (grad_hidden * gate_act).astype(jnp.bfloat16)
    part_gate = matmul(hidden_in.T, grad_gate_bf)
    part_up = matmul(hidden_in.T, grad_up_bf)
    grad_norm_mid = matmul(grad_gate_bf, back_gate.T) + matmul(grad_up_bf, back_up.T)
    back_mid, part_gffn = norm_back(grad_norm_mid, unit_mid, rms_mid, back_gffn)
    grad_gate, grad_up, grad_gffn = (
        lax.psum_scatter(
            part_gate.astype(jnp.bfloat16), "shard", scatter_dimension=0, tiled=True
        ).astype(jnp.float32),
        lax.psum_scatter(
            part_up.astype(jnp.bfloat16), "shard", scatter_dimension=0, tiled=True
        ).astype(jnp.float32),
        lax.psum_scatter(
            part_gffn.astype(jnp.bfloat16), "shard", scatter_dimension=0, tiled=True
        ).astype(jnp.float32),
    )
    grad_gate, grad_up, grad_gffn = (
        lax.psum(grad_gate.astype(jnp.bfloat16), "rep").astype(jnp.float32),
        lax.psum(grad_up.astype(jnp.bfloat16), "rep").astype(jnp.float32),
        lax.psum(grad_gffn.astype(jnp.bfloat16), "rep").astype(jnp.float32),
    )
    grad_mid = grad_y + back_mid
    grad_mid_bf = grad_mid.astype(jnp.bfloat16)
    again_set = (
        lax.all_gather(w_query, "shard", axis=0, tiled=True),
        lax.all_gather(w_key, "shard", axis=0, tiled=True),
        lax.all_gather(w_value, "shard", axis=0, tiled=True),
        lax.all_gather(w_out, "shard", axis=0, tiled=True),
        lax.all_gather(gain_attn, "shard", axis=0, tiled=True),
        lax.all_gather(gain_query, "shard", axis=0, tiled=True),
        lax.all_gather(gain_key, "shard", axis=0, tiled=True),
    )
    back_query, back_key, back_value, back_out, back_gattn, back_gquery, back_gkey = again_set
    part_out = matmul(mixed_bf.T, grad_mid_bf)
    grad_mixed_bf = (
        matmul(grad_mid_bf, back_out.T)
        .astype(jnp.bfloat16)
        .reshape(1, tok_rows, KVH, head_share, HEAD_DIM)
    )
    attn_again, unused_total = attn_probs_of(query_bf, key_bf, key_mask, log_total, score_scale)
    probs_bf = attn_again.astype(jnp.bfloat16)
    grad_scores = jnp.einsum(
        "gqkrd,gskd->gkrqs", grad_mixed_bf, value_bf, preferred_element_type=jnp.float32
    )
    grad_value_bf = (
        jnp.einsum("gkrqs,gqkrd->gskd", probs_bf, grad_mixed_bf, preferred_element_type=jnp.float32)
        .astype(jnp.bfloat16)
        .reshape(tok_rows, KVH * HEAD_DIM)
    )
    row_dot = jnp.sum(attn_again * grad_scores, axis=-1, keepdims=True)
    grad_logits = (attn_again * (grad_scores - row_dot) * score_scale).astype(jnp.bfloat16)
    grad_query_rot = jnp.einsum(
        "gkrqs,gskd->gqkrd", grad_logits, key_bf, preferred_element_type=jnp.float32
    ).reshape(1, tok_rows, QH, HEAD_DIM)
    grad_key_rot = jnp.einsum(
        "gkrqs,gqkrd->gskd", grad_logits, query_bf, preferred_element_type=jnp.float32
    )
    grad_query_raw, part_gquery = norm_back(
        rotate_back(grad_query_rot, cos_tab, sin_tab), query_unit, query_rms, back_gquery
    )
    grad_key_raw, part_gkey = norm_back(
        rotate_back(grad_key_rot, cos_tab, sin_tab), key_unit, key_rms, back_gkey
    )
    grad_query_bf = grad_query_raw.astype(jnp.bfloat16).reshape(tok_rows, QH * HEAD_DIM)
    grad_key_bf = grad_key_raw.astype(jnp.bfloat16).reshape(tok_rows, KVH * HEAD_DIM)
    part_query = matmul(normed_bf.T, grad_query_bf)
    part_key = matmul(normed_bf.T, grad_key_bf)
    part_value = matmul(normed_bf.T, grad_value_bf)
    grad_norm_in = (
        matmul(grad_query_bf, back_query.T)
        + matmul(grad_key_bf, back_key.T)
        + matmul(grad_value_bf, back_value.T)
    )
    back_in, part_gattn = norm_back(grad_norm_in, unit_in, rms_in, back_gattn)
    grad_tokens = grad_mid + back_in
    attn_grads = (
        lax.psum_scatter(
            part_query.astype(jnp.bfloat16), "shard", scatter_dimension=0, tiled=True
        ).astype(jnp.float32),
        lax.psum_scatter(
            part_key.astype(jnp.bfloat16), "shard", scatter_dimension=0, tiled=True
        ).astype(jnp.float32),
        lax.psum_scatter(
            part_value.astype(jnp.bfloat16), "shard", scatter_dimension=0, tiled=True
        ).astype(jnp.float32),
        lax.psum_scatter(
            part_out.astype(jnp.bfloat16), "shard", scatter_dimension=0, tiled=True
        ).astype(jnp.float32),
        lax.psum_scatter(
            part_gattn.astype(jnp.bfloat16), "shard", scatter_dimension=0, tiled=True
        ).astype(jnp.float32),
        lax.psum_scatter(
            part_gquery.astype(jnp.bfloat16), "shard", scatter_dimension=0, tiled=True
        ).astype(jnp.float32),
        lax.psum_scatter(
            part_gkey.astype(jnp.bfloat16), "shard", scatter_dimension=0, tiled=True
        ).astype(jnp.float32),
    )
    grad_query, grad_key, grad_value, grad_out, grad_gattn, grad_gquery, grad_gkey = attn_grads
    grad_query, grad_key, grad_value, grad_out, grad_gattn, grad_gquery, grad_gkey = (
        lax.psum(grad_query.astype(jnp.bfloat16), "rep").astype(jnp.float32),
        lax.psum(grad_key.astype(jnp.bfloat16), "rep").astype(jnp.float32),
        lax.psum(grad_value.astype(jnp.bfloat16), "rep").astype(jnp.float32),
        lax.psum(grad_out.astype(jnp.bfloat16), "rep").astype(jnp.float32),
        lax.psum(grad_gattn.astype(jnp.bfloat16), "rep").astype(jnp.float32),
        lax.psum(grad_gquery.astype(jnp.bfloat16), "rep").astype(jnp.float32),
        lax.psum(grad_gkey.astype(jnp.bfloat16), "rep").astype(jnp.float32),
    )
    return (
        block_out,
        grad_tokens,
        grad_query,
        grad_key,
        grad_value,
        grad_out,
        grad_gate,
        grad_up,
        grad_down,
        grad_gattn,
        grad_gffn,
        grad_gquery,
        grad_gkey,
    )


def solution(mesh):
    return jax.shard_map(
        local,
        mesh=mesh,
        in_specs=(
            P(("rep", "shard"), None),
            P(("rep", "shard"), None),
            P(("rep", "shard")),
            P("shard", None),
            P("shard", None),
            P("shard", None),
            P("shard", None),
            P("shard", None),
            P("shard", None),
            P("shard", None),
            P("shard"),
            P("shard"),
            P("shard"),
            P("shard"),
        ),
        out_specs=(
            P(("rep", "shard"), None),
            P(("rep", "shard"), None),
            P("shard", None),
            P("shard", None),
            P("shard", None),
            P("shard", None),
            P("shard", None),
            P("shard", None),
            P("shard", None),
            P("shard"),
            P("shard"),
            P("shard"),
            P("shard"),
        ),
        check_vma=False,
    )
```

profile of v0, /device:TPU:0, one launch (start us, length us, event | category | flops | bytes accessed | tf_op | source)
XLA Modules:
  0.0 995.9 jit_solution(12376034962835203929)
XLA Ops:
  12.0 6.0 all-gather
  19.8 8.2 all-reduce.9
  28.6 5.1 all-gather.1
  36.4 1.6 fusion.41
  38.2 9.2 all-gather.10.cloned.1.call-done
  47.4 1.6 convolution_convert_fusion.9
  49.2 0.8 copy.95
  50.8 20.9 %all-gather.14.cloned.1.call-done = bf16[1024,1024]{1,0:T(8,128)(2,1)} async-done(((bf16[256,1024]{1,0:T(8,128)(2,1)}), bf16[1024,1024]{1,0:T(8,128)(2,1)}) %all-gather.14.cloned.1.call-update) | async-done | bytes 2097168 | tf_op jit(solution)/shard_map/all_gather | solution.py:105
  71.7 2.1 fusion.39
  75.9 19.7 %all-gather.16.cloned.1.call-done = bf16[1024,1024]{1,0:T(8,128)(2,1)} async-done(((bf16[256,1024]{1,0:T(8,128)(2,1)}), bf16[1024,1024]{1,0:T(8,128)(2,1)}) %all-gather.16.cloned.1.call-update) | async-done | bytes 2097168 | tf_op jit(solution)/shard_map/all_gather | solution.py:108
  95.7 2.1 multiply_reduce_fusion.5
  98.0 63.3 %all-gather.18.cloned.1.call-done = bf16[1024,4608]{1,0:T(8,128)(2,1)} async-done(((bf16[256,4608]{1,0:T(8,128)(2,1)}), bf16[1024,4608]{1,0:T(8,128)(2,1)}) %all-gather.18.cloned.1.call-update) | async-done | bytes 9437200 | tf_op jit(solution)/shard_map/all_gather | solution.py:143
  161.3 6.5 fusion.45
  167.8 59.2 %all-gather.20.cloned.1.call-done = bf16[1024,4608]{1,0:T(8,128)(2,1)} async-done(((bf16[256,4608]{1,0:T(8,128)(2,1)}), bf16[1024,4608]{1,0:T(8,128)(2,1)}) %all-gather.20.cloned.1.call-update) | async-done | bytes 9437200 | tf_op jit(solution)/shard_map/all_gather | solution.py:144
  227.0 6.5 fusion.46
  233.5 59.3 %all-gather.22.cloned.1.call-done = bf16[4608,1024]{1,0:T(8,128)(2,1)} async-done(((bf16[1152,1024]{1,0:T(8,128)(2,1)}), bf16[4608,1024]{1,0:T(8,128)(2,1)}) %all-gather.22.cloned.1.call-update) | async-done | bytes 9437200 | tf_op jit(solution)/shard_map/all_gather | solution.py:145
  292.8 8.8 multiply_convert_fusion
  301.6 7.6 fusion.47
  309.3 3.7 multiply_reduce_fusion.2
  313.3 0.8 copy-done.5
  314.0 1.7 convolution_convert_fusion.7
  315.7 1.8 copy.85
  317.5 1.4 multiply_reduce_fusion
  319.4 0.8 copy-done.11
  320.5 0.7 pad_maximum_fusion.2
  321.3 0.7 mul.600
  322.0 1.8 copy.94
  323.8 1.8 copy.92
  325.6 1.9 multiply_reduce_fusion.7
  328.2 2.2 convolution_convert_fusion.6
  330.4 1.0 fusion.3
  332.1 2.2 convolution_convert_fusion.5
  335.1 0.8 mul.567
  335.9 2.0 copy.90
  338.3 0.9 pad_maximum_fusion
  339.3 1.0 copy.89
  340.3 1.2 copy.87
  341.6 1.4 multiply_reduce_fusion.1
  343.0 2.1 convolution_convert_fusion.4
  345.2 2.0 convolution_convert_fusion.3
  347.3 6.4 convolution_convert_fusion.2
  353.8 6.3 convolution_convert_fusion.1
  360.2 0.9 copy-done.26
  361.1 5.3 convolution_convert_fusion
  366.4 16.8 %reduce-scatter.12.cloned.1.call-done = bf16[256,512]{1,0:T(8,128)(2,1)} async-done(((bf16[1024,512]{1,0:T(8,128)(2,1)}), bf16[256,512]{1,0:T(8,128)(2,1)}) %reduce-scatter.12.cloned.1.call-update) | async-done | bytes 262160 | tf_op jit(solution)/shard_map/reduce_scatter | solution.py:257
  383.3 34.1 %reduce-scatter.8.cloned.1.call-done = bf16[256,1024]{1,0:T(8,128)(2,1)} async-done(((bf16[1024,1024]{1,0:T(8,128)(2,1)}), bf16[256,1024]{1,0:T(8,128)(2,1)}) %reduce-scatter.8.cloned.1.call-update) | async-done | bytes 524304 | tf_op jit(solution)/shard_map/reduce_scatter | solution.py:251
  417.4 34.3 %reduce-scatter.14.cloned.1.call-done = bf16[256,1024]{1,0:T(8,128)(2,1)} async-done(((bf16[1024,1024]{1,0:T(8,128)(2,1)}), bf16[256,1024]{1,0:T(8,128)(2,1)}) %reduce-scatter.14.cloned.1.call-update) | async-done | bytes 524304 | tf_op jit(solution)/shard_map/reduce_scatter | solution.py:260
  451.7 80.4 %reduce-scatter.16.cloned.1.call-done = bf16[256,4608]{1,0:T(8,128)(2,1)} async-done(((bf16[1024,4608]{1,0:T(8,128)(2,1)}), bf16[256,4608]{1,0:T(8,128)(2,1)}) %reduce-scatter.16.cloned.1.call-update) | async-done | bytes 2359312 | tf_op jit(solution)/shard_map/reduce_scatter | solution.py:181
  532.1 80.5 %reduce-scatter.18.cloned.1.call-done = bf16[256,4608]{1,0:T(8,128)(2,1)} async-done(((bf16[1024,4608]{1,0:T(8,128)(2,1)}), bf16[256,4608]{1,0:T(8,128)(2,1)}) %reduce-scatter.18.cloned.1.call-update) | async-done | bytes 2359312 | tf_op jit(solution)/shard_map/reduce_scatter | solution.py:184
  612.6 80.4 %reduce-scatter.20.cloned.1.call-done = bf16[1152,1024]{1,0:T(8,128)(2,1)} async-done(((bf16[4608,1024]{1,0:T(8,128)(2,1)}), bf16[1152,1024]{1,0:T(8,128)(2,1)}) %reduce-scatter.20.cloned.1.call-update) | async-done | bytes 2359312 | tf_op jit(solution)/shard_map/reduce_scatter | solution.py:167
  694.6 2.5 fusion.48
  697.1 1.7 convolution_add_fusion.1
  699.5 5.8 all-reduce.8
  705.6 23.1 %all-reduce.6 = (bf16[256]{0:T(256)(128)(2,1)S(1)}, bf16[256]{0:T(256)(128)(2,1)S(1)}, bf16[16]{0:T(256)(128)(2,1)S(1)}, bf16[16]{0:T(256)(128)(2,1)S(1)}) all-reduce(bf16[256]{0:T(256)(128)(2,1)S(1)} %dynamic-slice.3, bf16[256]{0:T(256)(128)(2,1)S(1)} %dynamic-slice.5, ...), channel_id=1, replica_groups=mesh['rep'=8,'shard'=4] {'rep'}, use_global_device_ids=true, to_apply=%region_27.28 | all-reduce | flops 544 | bytes 2176 | tf_op jit(solution)/shard_map/psum | solution.py:279
  730.9 1.0 fusion.14
  731.9 5.8 fusion.2
  737.7 237.7 %all-reduce.12.cloned.1.call-done = (bf16[256,1024]{1,0:T(8,128)(2,1)}, bf16[256,512]{1,0:T(8,128)(2,1)}, bf16[256,512]{1,0:T(8,128)(2,1)}, bf16[256,1024]{1,0:T...) async-done(((bf16[256,1024]{1,0:T(8,128)(2,1)}, bf16[256,512]{1,0:T(8,128)(2,1)}, bf16[256,512]{1,0:T(8,128)(2,1)}, ...) | async-done | bytes 8650768 | tf_op jit(solution)/shard_map/psum | solution.py:275
  975.5 4.6 convert_element_type.257
  980.0 2.7 convert_element_type.259
  982.8 2.7 convert_element_type.261
  985.5 1.1 convert_element_type.249
  986.6 1.1 convert_element_type.255
  987.7 0.9 convert_element_type.251
  988.5 0.9 convert_element_type.253
  (243 shorter events, 19.2 us)
Async XLA Ops:
  7.2 29.2 %all-gather.12.cloned.1.call-start = ((), (), s32[]{:S(2)}) async-start(), calls=%async_computation.8 | async-start | bytes 1310720 | tf_op jit(solution)/shard_map/all_gather | solution.py:106
  7.9 39.5 %all-gather.10.cloned.1.call-start = ((), (), s32[]{:S(2)}) async-start(), calls=%async_computation.7 | async-start | bytes 1310720 | tf_op jit(solution)/shard_map/all_gather | solution.py:107
  8.7 63.0 %all-gather.14.cloned.1.call-start = ((), (), s32[]{:S(2)}) async-start(), calls=%async_computation.9 | async-start | bytes 2621440 | tf_op jit(solution)/shard_map/all_gather | solution.py:105
  9.4 86.3 %all-gather.16.cloned.1.call-start = ((), (), s32[]{:S(2)}) async-start(), calls=%async_computation.10 | async-start | bytes 2621440 | tf_op jit(solution)/shard_map/all_gather | solution.py:108
  10.0 151.3 %all-gather.18.cloned.1.call-start = ((), (), s32[]{:S(2)}) async-start(), calls=%async_computation.11 | async-start | bytes 11796480 | tf_op jit(solution)/shard_map/all_gather | solution.py:143
  10.6 7.5 copy-start.66
  10.6 8.7 copy-start.72
  10.6 9.0 copy-start.73
  10.6 17.4 %copy-start.65 = (s32[128]{0:T(128)S(1)}, s32[128]{0:T(128)}, u32[]{:S(2)}) copy-start(s32[128]{0:T(128)} %param.16) | copy-start | bytes 1540
  10.6 17.9 %copy-start.74 = (bf16[256]{0:T(256)(128)(2,1)S(1)}, bf16[256]{0:T(256)(128)(2,1)}, u32[]{:S(2)}) copy-start(bf16[256]{0:T(256)(128)(2,1)} %param.25) | copy-start | bytes 1540
  10.6 24.3 %copy-start.1 = (bf16[128,1024]{1,0:T(8,128)(2,1)S(1)}, bf16[128,1024]{1,0:T(8,128)(2,1)}, u32[]{:S(2)}) copy-start(bf16[128,1024]{1,0:T(8,128)(2,1)} %param.14) | copy-start | bytes 786436
  10.6 216.3 %all-gather.20.cloned.1.call-start = ((), (), s32[]{:S(2)}) async-start(), calls=%async_computation.12 | async-start | bytes 11796480 | tf_op jit(solution)/shard_map/all_gather | solution.py:144
  11.2 281.6 %all-gather.22.cloned.1.call-start = ((), (), s32[]{:S(2)}) async-start(), calls=%async_computation.13 | async-start | bytes 11796480 | tf_op jit(solution)/shard_map/all_gather | solution.py:145
  12.0 354.5 %reduce-scatter.10.cloned.1.call-start = ((), (), s32[]{:S(2)}) async-start(), calls=%async_computation.15 | async-start | bytes 1310720 | tf_op jit(solution)/shard_map/reduce_scatter | solution.py:254
  18.1 53.6 %copy-start.38 = (f32[4,1,256]{2,1,0:T(1,128)}, f32[4,1,256]{2,1,0:T(1,128)S(1)}, u32[]{:S(2)}) copy-start(f32[4,1,256]{2,1,0:T(1,128)S(1)} %convert_element_type.270) | copy-start | bytes 12292
  28.1 46.0 %copy-start.63 = (f32[64]{0:T(128)}, f32[64]{0:T(128)S(1)}, u32[]{:S(2)}) copy-start(f32[64]{0:T(128)S(1)} %convert_element_type.226) | copy-start | bytes 772
  28.5 21.5 %copy-start.67 = (f32[64]{0:T(128)}, f32[64]{0:T(128)S(1)}, u32[]{:S(2)}) copy-start(f32[64]{0:T(128)S(1)} %convert_element_type.222) | copy-start | bytes 772
  35.5 36.1 %copy-start.54 = (f32[128]{0:T(128)}, f32[128]{0:T(128)S(1)}, u32[]{:S(2)}) copy-start(f32[128]{0:T(128)S(1)} %add_rsqrt_fusion.3) | copy-start | bytes 1540
  36.4 38.4 %copy-start.33 = (f32[128,32]{0,1:T(8,128)}, f32[128,32]{0,1:T(8,128)S(1)}, u32[]{:S(2)}) copy-start(f32[128,32]{0,1:T(8,128)S(1)} %get-tuple-element.54) | copy-start | bytes 49156
  38.1 35.7 %copy-start.17 = (f32[128,512]{1,0:T(8,128)}, f32[128,512]{1,0:T(8,128)S(1)}, u32[]{:S(2)}) copy-start(f32[128,512]{1,0:T(8,128)S(1)} %fusion.41) | copy-start | bytes 786436
  49.1 26.5 %copy-start.20 = (bf16[128,512]{0,1:T(8,128)(2,1)}, bf16[128,512]{0,1:T(8,128)(2,1)S(1)}, u32[]{:S(2)}) copy-start(bf16[128,512]{0,1:T(8,128)(2,1)S(1)} %copy.81) | copy-start | bytes 393220
  49.1 24.8 %copy-start.52 = (f32[128,8]{0,1:T(8,128)}, f32[128,8]{0,1:T(8,128)S(1)}, u32[]{:S(2)}) copy-start(f32[128,8]{0,1:T(8,128)S(1)} %add_rsqrt_fusion.1) | copy-start | bytes 12292
  75.5 22.4 %copy-start.50 = (f32[4,1,256]{2,1,0:T(1,128)S(1)}, f32[4,1,256]{2,1,0:T(1,128)}, u32[]{:S(2)}) copy-start(f32[4,1,256]{2,1,0:T(1,128)} %convert_element_type.271) | copy-start | bytes 12292
  75.5 22.5 %copy-start.46 = (f32[8,2,128]{2,1,0:T(2,128)}, f32[8,2,128]{2,1,0:T(2,128)S(1)}, u32[]{:S(2)}) copy-start(f32[8,2,128]{2,1,0:T(2,128)S(1)} %log.8) | copy-start | bytes 24580
  75.9 21.9 %copy-start.18 = (bf16[8,64,2,128]{3,1,2,0:T(8,128)(2,1)}, bf16[8,64,2,128]{3,1,2,0:T(8,128)(2,1)S(1)}, u32[]{:S(2)}) copy-start(bf16[8,64,2,128]{3,1,2,0:T(8,128)(2,1)S(1)} %convolution_convert_fusion.8) | copy-start | bytes 786436
  97.8 70.0 %copy-start.59 = (f32[128]{0:T(128)}, f32[128]{0:T(128)S(1)}, u32[]{:S(2)}) copy-start(f32[128]{0:T(128)S(1)} %add_rsqrt_fusion.2) | copy-start | bytes 1540
  301.5 7.7 copy-start.8
  301.6 7.7 copy-start.7
  301.6 7.7 copy-start
  301.6 7.7 copy-start.51
  301.6 7.7 copy-start.60
  309.3 3.8 copy-start.25
  309.3 3.7 copy-start.61
  309.3 4.7 copy-start.2
  317.5 2.6 copy-start.30
  317.5 2.6 copy-start.32
  322.0 8.4 copy-start.16
  330.4 52.9 %reduce-scatter.12.cloned.1.call-start = ((), (), s32[]{:S(2)}) async-start(), calls=%async_computation.16 | async-start | bytes 1310720 | tf_op jit(solution)/shard_map/reduce_scatter | solution.py:257
  331.5 2.9 copy-start.70
  331.5 3.6 copy-start.49
  331.5 6.4 copy-start.12
  331.5 6.4 copy-start.43
  331.5 6.4 copy-start.45
  332.1 6.1 copy-start.35
  334.3 4.0 copy-start.4
  334.3 4.0 copy-start.64
  334.3 83.1 %reduce-scatter.8.cloned.1.call-start = ((), (), s32[]{:S(2)}) async-start(), calls=%async_computation.14 | async-start | bytes 2621440 | tf_op jit(solution)/shard_map/reduce_scatter | solution.py:251
  338.3 3.3 copy-start.10
  338.3 3.3 copy-start.56
  339.3 3.7 copy-start.39
  339.3 3.7 copy-start.55
  345.2 106.5 %reduce-scatter.14.cloned.1.call-start = ((), (), s32[]{:S(2)}) async-start(), calls=%async_computation.17 | async-start | bytes 2621440 | tf_op jit(solution)/shard_map/reduce_scatter | solution.py:260
  347.3 184.8 %reduce-scatter.16.cloned.1.call-start = ((), (), s32[]{:S(2)}) async-start(), calls=%async_computation.18 | async-start | bytes 11796480 | tf_op jit(solution)/shard_map/reduce_scatter | solution.py:181
  353.7 258.9 %reduce-scatter.18.cloned.1.call-start = ((), (), s32[]{:S(2)}) async-start(), calls=%async_computation.19 | async-start | bytes 11796480 | tf_op jit(solution)/shard_map/reduce_scatter | solution.py:184
  360.2 332.9 %reduce-scatter.20.cloned.1.call-start = ((), (), s32[]{:S(2)}) async-start(), calls=%async_computation.20 | async-start | bytes 11796480 | tf_op jit(solution)/shard_map/reduce_scatter | solution.py:167
  366.4 609.1 %all-reduce.12.cloned.1.call-start = ((), (), s32[]{:S(2)}) async-start(), calls=%async_computation.21 | async-start | bytes 17301504 | tf_op jit(solution)/shard_map/psum | solution.py:275
  693.1 4.1 copy-start.22
  694.6 4.3 copy-start.13
  694.6 4.3 copy-start.24
  975.5 4.6 copy-start.15
  980.0 2.7 copy-start.14
  982.8 2.7 copy-start.28
  982.8 3.8 copy-start.27
  985.5 3.0 copy-start.40
  (26 other events, 33.1 us)
Sparse Core Ops, SparseCore 0:
  9.5 19.4 all-gather.11
  30.6 16.6 all-gather.9
  48.9 22.6 all-gather.13
  73.1 22.5 all-gather.15
  97.1 64.2 all-gather.17
  162.7 64.2 all-gather.19
  228.5 64.2 all-gather.21
  330.5 24.8 reduce-scatter.9
  358.5 24.7 reduce-scatter.11
  386.2 31.1 reduce-scatter.7
  420.5 31.1 reduce-scatter.13
  454.2 77.8 reduce-scatter.15
  534.7 77.8 reduce-scatter.17
  615.1 77.8 reduce-scatter.19
  698.4 277.0 all-reduce.11
where the time goes:
time: 997 us; the launch traced here: 996 us
  waiting for transfers between devices  800 us (80%)
  matrix products  83.1 us (8%)
  blocking collectives  48.2 us (5%)
  other arithmetic  26.1 us (3%)
  local copies, waits for them, and re-layouts  20.5 us (2%)
  between operations  17 us (2%)
    psum x1, waiting for transfers between devices, local(): lax.psum(grad_query.astype(jnp.bfloat16), 'rep').astype(jnp.float32)  238 us
    reduce_scatter x1, waiting for transfers between devices, local(): lax.psum_scatter(part_up.astype(jnp.bfloat16), 'shard', scatter_dimension...  80.5 us
    reduce_scatter x1, waiting for transfers between devices, local(): lax.psum_scatter(part_gate.astype(jnp.bfloat16), 'shard', scatter_dimensi...  80.4 us
    reduce_scatter x1, waiting for transfers between devices, local(): lax.psum_scatter(part_down.astype(jnp.bfloat16), 'shard', scatter_dimensi...  80.4 us
    dot_general x21, matrix products, matmul(): return jnp.dot(left, right, preferred_element_type=jnp.float32)  79.3 us
    all_gather x1, waiting for transfers between devices, local(): lax.all_gather(w_gate, 'shard', axis=0, tiled=True)  63.3 us
    all_gather x1, waiting for transfers between devices, local(): lax.all_gather(w_down, 'shard', axis=0, tiled=True)  59.3 us
    all_gather x1, waiting for transfers between devices, local(): lax.all_gather(w_up, 'shard', axis=0, tiled=True)  59.2 us
  transfers between devices with their start and end apart: 15, of which 13 were waited for; matrix products, arithmetic and copies ran while one was open for 8% of the time, Pallas kernels for 0%

commit v1 on v0

--- a/solution.py
+++ b/solution.py
@@ -271,8 +271,11 @@
         ).astype(jnp.float32),
     )
     grad_query, grad_key, grad_value, grad_out, grad_gattn, grad_gquery, grad_gkey = attn_grads
+    work_sector_all = lambda array_here, named_axis: jax.lax.all_gather(
+        array_here, axis_name=named_axis
+    ).sum(axis=0)
     grad_query, grad_key, grad_value, grad_out, grad_gattn, grad_gquery, grad_gkey = (
-        lax.psum(grad_query.astype(jnp.bfloat16), "rep").astype(jnp.float32),
+        work_sector_all(grad_query.astype(jnp.bfloat16), "rep").astype(jnp.float32),
         lax.psum(grad_key.astype(jnp.bfloat16), "rep").astype(jnp.float32),
         lax.psum(grad_value.astype(jnp.bfloat16), "rep").astype(jnp.float32),
         lax.psum(grad_out.astype(jnp.bfloat16), "rep").astype(jnp.float32),

time: 997 us -> 1060 us (1.063)
  waiting for transfers between devices: 800 us -> 848 us
    reduce_scatter x1, waiting for transfers between devices: 34.1 us -> 0.02 us  [local(): lax.psum_scatter(part_query.astype(jnp.bfloat16), 'shard', scatter_dimens...]
    all_gather x0 -> x1, waiting for transfers between devices: none -> 31.2 us  [local(): jax.lax.all_gather(array_here, axis_name=named_axis).sum(axis=0)]
    psum x1, waiting for transfers between devices: 238 us -> 262 us  [local(): lax.psum(grad_key.astype(jnp.bfloat16), 'rep').astype(jnp.float32)]
    reduce_scatter x1, waiting for transfers between devices: 0.02 us -> 15 us  [local(): lax.psum_scatter(part_key.astype(jnp.bfloat16), 'shard', scatter_dimensio...]
    reduce_scatter x1, waiting for transfers between devices: 16.8 us -> 27.7 us  [local(): lax.psum_scatter(part_value.astype(jnp.bfloat16), 'shard', scatter_dimens...]
  transfers between devices with their start and end apart: 15 -> 16, of which waited for: 13 -> 14; matrix products, arithmetic and copies ran while one was open for 8% -> 8% of each run, Pallas kernels for 0% -> 0%
where the time goes in v1:
time: 1060 us; the launch traced here: 1050 us
  waiting for transfers between devices  848 us (80%)
  matrix products  84.2 us (8%)
  blocking collectives  47.4 us (4%)
  other arithmetic  31.5 us (3%)
  local copies, waits for them, and re-layouts  25.8 us (2%)
  between operations  16.9 us (2%)
    psum x1, waiting for transfers between devices, local(): lax.psum(grad_key.astype(jnp.bfloat16), 'rep').astype(jnp.float32)  262 us
    reduce_scatter x1, waiting for transfers between devices, local(): lax.psum_scatter(part_up.astype(jnp.bfloat16), 'shard', scatter_dimension...  80.6 us
    reduce_scatter x1, waiting for transfers between devices, local(): lax.psum_scatter(part_gate.astype(jnp.bfloat16), 'shard', scatter_dimensi...  80.4 us
    reduce_scatter x1, waiting for transfers between devices, local(): lax.psum_scatter(part_down.astype(jnp.bfloat16), 'shard', scatter_dimensi...  80.4 us
    dot_general x21, matrix products, matmul(): return jnp.dot(left, right, preferred_element_type=jnp.float32)  79.3 us
    all_gather x1, waiting for transfers between devices, local(): lax.all_gather(w_gate, 'shard', axis=0, tiled=True)  63.4 us
    all_gather x1, waiting for transfers between devices, local(): lax.all_gather(w_down, 'shard', axis=0, tiled=True)  59.3 us
    all_gather x1, waiting for transfers between devices, local(): lax.all_gather(w_up, 'shard', axis=0, tiled=True)  59.2 us
  transfers between devices with their start and end apart: 16, of which 14 were waited for; matrix products, arithmetic and copies ran while one was open for 8% of the time, Pallas kernels for 0%

profile of v1, /device:TPU:0, one launch (start us, length us, event | category | flops | bytes accessed | tf_op | source)
XLA Modules:
  0.0 1054.9 jit_solution(10964151992335791158)
XLA Ops:
  12.0 6.0 all-gather.1
  19.8 8.2 all-reduce.9
  28.6 5.1 all-gather.2
  36.5 1.6 fusion.41
  38.2 9.1 all-gather.12.cloned.1.call-done
  47.4 1.6 convolution_convert_fusion.9
  50.0 21.6 %all-gather.16.cloned.1.call-done = bf16[1024,1024]{1,0:T(8,128)(2,1)} async-done(((bf16[256,1024]{1,0:T(8,128)(2,1)}), bf16[1024,1024]{1,0:T(8,128)(2,1)}) %all-gather.16.cloned.1.call-update) | async-done | bytes 2097168 | tf_op jit(solution)/shard_map/all_gather | solution.py:105
  71.5 2.1 fusion.39
  75.5 1.0 copy.90
  76.8 18.7 %all-gather.18.cloned.1.call-done = bf16[1024,1024]{1,0:T(8,128)(2,1)} async-done(((bf16[256,1024]{1,0:T(8,128)(2,1)}), bf16[1024,1024]{1,0:T(8,128)(2,1)}) %all-gather.18.cloned.1.call-update) | async-done | bytes 2097168 | tf_op jit(solution)/shard_map/all_gather | solution.py:108
  95.6 2.1 multiply_reduce_fusion.5
  97.9 63.4 %all-gather.20.cloned.1.call-done = bf16[1024,4608]{1,0:T(8,128)(2,1)} async-done(((bf16[256,4608]{1,0:T(8,128)(2,1)}), bf16[1024,4608]{1,0:T(8,128)(2,1)}) %all-gather.20.cloned.1.call-update) | async-done | bytes 9437200 | tf_op jit(solution)/shard_map/all_gather | solution.py:143
  161.2 6.5 fusion.45
  167.7 59.2 %all-gather.22.cloned.1.call-done = bf16[1024,4608]{1,0:T(8,128)(2,1)} async-done(((bf16[256,4608]{1,0:T(8,128)(2,1)}), bf16[1024,4608]{1,0:T(8,128)(2,1)}) %all-gather.22.cloned.1.call-update) | async-done | bytes 9437200 | tf_op jit(solution)/shard_map/all_gather | solution.py:144
  226.9 6.5 fusion.46
  233.4 59.3 %all-gather.24.cloned.1.call-done = bf16[4608,1024]{1,0:T(8,128)(2,1)} async-done(((bf16[1152,1024]{1,0:T(8,128)(2,1)}), bf16[4608,1024]{1,0:T(8,128)(2,1)}) %all-gather.24.cloned.1.call-update) | async-done | bytes 9437200 | tf_op jit(solution)/shard_map/all_gather | solution.py:145
  292.7 8.8 multiply_convert_fusion
  301.5 7.6 fusion.47
  309.2 3.7 multiply_reduce_fusion.2
  314.0 1.7 convolution_convert_fusion.7
  315.7 1.8 copy.85
  317.5 1.4 multiply_reduce_fusion
  320.0 0.9 pad_maximum_fusion
  321.8 2.0 copy.89
  323.8 2.0 copy.87
  325.8 2.3 multiply_reduce_fusion.1
  328.9 2.1 convolution_convert_fusion.4
  331.1 1.2 mul.593
  332.3 1.3 mul.594
  333.7 1.4 mul.587
  335.1 1.8 copy.95
  336.8 1.5 convolution_bitcast_fusion.2
  339.1 1.4 pad_maximum_fusion.2
  341.2 1.8 copy.94
  343.1 1.8 copy.92
  344.9 1.8 multiply_reduce_fusion.7
  347.3 2.2 convolution_convert_fusion.6
  349.6 1.0 fusion.3
  351.3 2.2 convolution_convert_fusion.5
  353.6 2.0 convolution_convert_fusion.3
  355.7 6.4 convolution_convert_fusion.2
  362.1 6.4 convolution_convert_fusion.1
  368.5 0.9 copy-done.26
  369.4 5.3 convolution_convert_fusion
  375.3 15.0 %reduce-scatter.10.cloned.1.call-done = bf16[256,512]{1,0:T(8,128)(2,1)} async-done(((bf16[1024,512]{1,0:T(8,128)(2,1)}), bf16[256,512]{1,0:T(8,128)(2,1)}) %reduce-scatter.10.cloned.1.call-update) | async-done | bytes 262160 | tf_op jit(solution)/shard_map/reduce_scatter | solution.py:254
  390.3 27.7 %reduce-scatter.12.cloned.1.call-done = bf16[256,512]{1,0:T(8,128)(2,1)} async-done(((bf16[1024,512]{1,0:T(8,128)(2,1)}), bf16[256,512]{1,0:T(8,128)(2,1)}) %reduce-scatter.12.cloned.1.call-update) | async-done | bytes 262160 | tf_op jit(solution)/shard_map/reduce_scatter | solution.py:257
  418.1 34.3 %reduce-scatter.14.cloned.1.call-done = bf16[256,1024]{1,0:T(8,128)(2,1)} async-done(((bf16[1024,1024]{1,0:T(8,128)(2,1)}), bf16[256,1024]{1,0:T(8,128)(2,1)}) %reduce-scatter.14.cloned.1.call-update) | async-done | bytes 524304 | tf_op jit(solution)/shard_map/reduce_scatter | solution.py:260
  452.4 80.4 %reduce-scatter.16.cloned.1.call-done = bf16[256,4608]{1,0:T(8,128)(2,1)} async-done(((bf16[1024,4608]{1,0:T(8,128)(2,1)}), bf16[256,4608]{1,0:T(8,128)(2,1)}) %reduce-scatter.16.cloned.1.call-update) | async-done | bytes 2359312 | tf_op jit(solution)/shard_map/reduce_scatter | solution.py:181
  532.8 80.6 %reduce-scatter.18.cloned.1.call-done = bf16[256,4608]{1,0:T(8,128)(2,1)} async-done(((bf16[1024,4608]{1,0:T(8,128)(2,1)}), bf16[256,4608]{1,0:T(8,128)(2,1)}) %reduce-scatter.18.cloned.1.call-update) | async-done | bytes 2359312 | tf_op jit(solution)/shard_map/reduce_scatter | solution.py:184
  613.4 80.4 %reduce-scatter.20.cloned.1.call-done = bf16[1152,1024]{1,0:T(8,128)(2,1)} async-done(((bf16[4608,1024]{1,0:T(8,128)(2,1)}), bf16[1152,1024]{1,0:T(8,128)(2,1)}) %reduce-scatter.20.cloned.1.call-update) | async-done | bytes 2359312 | tf_op jit(solution)/shard_map/reduce_scatter | solution.py:167
  695.4 2.5 fusion.48
  698.0 1.7 convolution_add_fusion.1
  700.3 5.8 all-reduce.8
  706.5 22.3 %all-reduce.6 = (bf16[256]{0:T(256)(128)(2,1)S(1)}, bf16[256]{0:T(256)(128)(2,1)S(1)}, bf16[16]{0:T(256)(128)(2,1)S(1)}, bf16[16]{0:T(256)(128)(2,1)S(1)}) all-reduce(bf16[256]{0:T(256)(128)(2,1)S(1)} %dynamic-slice.3, bf16[256]{0:T(256)(128)(2,1)S(1)} %dynamic-slice.5, ...), channel_id=1, replica_groups=mesh['rep'=8,'shard'=4] {'rep'}, use_global_device_ids=true, to_apply=%region_27.28 | all-reduce | flops 544 | bytes 2176 | tf_op jit(solution)/shard_map/psum | solution.py:282
  730.9 1.0 fusion.14
  731.9 5.8 fusion.2
  737.7 31.2 %all-gather.26.cloned.1.call-done = bf16[2048,1024]{1,0:T(8,128)(2,1)} async-done(((bf16[256,1024]{1,0:T(8,128)(2,1)}), bf16[2048,1024]{1,0:T(8,128)(2,1)}) %all-gather.26.cloned.1.call-update) | async-done | bytes 4194320 | tf_op jit(solution)/shard_map/all_gather | solution.py:274
  768.9 3.1 reduce_sum.172
  772.0 1.1 convert_element_type.251
  773.1 262.5 %all-reduce.12.cloned.1.call-done = (bf16[256,512]{1,0:T(8,128)(2,1)}, bf16[256,512]{1,0:T(8,128)(2,1)}, bf16[256,1024]{1,0:T(8,128)(2,1)}, bf16[256,4608]{1,0:T...) async-done(((bf16[256,512]{1,0:T(8,128)(2,1)}, bf16[256,512]{1,0:T(8,128)(2,1)}, bf16[256,1024]{1,0:T(8,128)(2,1)}, bf16[256,4608]{1,0:T(8,128)(2,1)}, ...) | async-done | bytes 8126480 | tf_op jit(solution)/shard_map/psum | solution.py:279
  1035.6 4.6 convert_element_type.259
  1040.1 2.7 convert_element_type.261
  1042.9 2.7 convert_element_type.263
  1045.6 1.1 convert_element_type.257
  (241 shorter events, 24.6 us)
Async XLA Ops:
  7.2 29.3 %all-gather.14.cloned.1.call-start = ((), (), s32[]{:S(2)}) async-start(), calls=%async_computation.8 | async-start | bytes 1310720 | tf_op jit(solution)/shard_map/all_gather | solution.py:106
  7.9 39.5 %all-gather.12.cloned.1.call-start = ((), (), s32[]{:S(2)}) async-start(), calls=%async_computation.7 | async-start | bytes 1310720 | tf_op jit(solution)/shard_map/all_gather | solution.py:107
  8.7 62.9 %all-gather.16.cloned.1.call-start = ((), (), s32[]{:S(2)}) async-start(), calls=%async_computation.9 | async-start | bytes 2621440 | tf_op jit(solution)/shard_map/all_gather | solution.py:105
  9.4 86.2 %all-gather.18.cloned.1.call-start = ((), (), s32[]{:S(2)}) async-start(), calls=%async_computation.10 | async-start | bytes 2621440 | tf_op jit(solution)/shard_map/all_gather | solution.py:108
  10.0 151.2 %all-gather.20.cloned.1.call-start = ((), (), s32[]{:S(2)}) async-start(), calls=%async_computation.11 | async-start | bytes 11796480 | tf_op jit(solution)/shard_map/all_gather | solution.py:143
  10.6 7.5 copy-start.65
  10.6 8.7 copy-start.69
  10.6 9.0 copy-start.70
  10.6 17.4 %copy-start.64 = (s32[128]{0:T(128)S(1)}, s32[128]{0:T(128)}, u32[]{:S(2)}) copy-start(s32[128]{0:T(128)} %param.16) | copy-start | bytes 1540
  10.6 18.0 %copy-start.71 = (bf16[256]{0:T(256)(128)(2,1)S(1)}, bf16[256]{0:T(256)(128)(2,1)}, u32[]{:S(2)}) copy-start(bf16[256]{0:T(256)(128)(2,1)} %param.25) | copy-start | bytes 1540
  10.6 24.3 %copy-start.1 = (bf16[128,1024]{1,0:T(8,128)(2,1)S(1)}, bf16[128,1024]{1,0:T(8,128)(2,1)}, u32[]{:S(2)}) copy-start(bf16[128,1024]{1,0:T(8,128)(2,1)} %param.14) | copy-start | bytes 786436
  10.6 216.2 %all-gather.22.cloned.1.call-start = ((), (), s32[]{:S(2)}) async-start(), calls=%async_computation.12 | async-start | bytes 11796480 | tf_op jit(solution)/shard_map/all_gather | solution.py:144
  11.2 281.5 %all-gather.24.cloned.1.call-start = ((), (), s32[]{:S(2)}) async-start(), calls=%async_computation.13 | async-start | bytes 11796480 | tf_op jit(solution)/shard_map/all_gather | solution.py:145
  12.0 362.8 %reduce-scatter.8.cloned.1.call-start = ((), (), s32[]{:S(2)}) async-start(), calls=%async_computation.14 | async-start | bytes 2621440 | tf_op jit(solution)/shard_map/reduce_scatter | solution.py:251
  18.1 53.5 %copy-start.36 = (f32[4,1,256]{2,1,0:T(1,128)}, f32[4,1,256]{2,1,0:T(1,128)S(1)}, u32[]{:S(2)}) copy-start(f32[4,1,256]{2,1,0:T(1,128)S(1)} %convert_element_type.272) | copy-start | bytes 12292
  28.1 45.9 %copy-start.62 = (f32[64]{0:T(128)}, f32[64]{0:T(128)S(1)}, u32[]{:S(2)}) copy-start(f32[64]{0:T(128)S(1)} %convert_element_type.228) | copy-start | bytes 772
  28.6 20.7 %copy-start.66 = (f32[64]{0:T(128)}, f32[64]{0:T(128)S(1)}, u32[]{:S(2)}) copy-start(f32[64]{0:T(128)S(1)} %convert_element_type.224) | copy-start | bytes 772
  35.6 36.0 %copy-start.52 = (f32[128]{0:T(128)}, f32[128]{0:T(128)S(1)}, u32[]{:S(2)}) copy-start(f32[128]{0:T(128)S(1)} %add_rsqrt_fusion.3) | copy-start | bytes 1540
  36.4 37.7 %copy-start.30 = (f32[128,32]{0,1:T(8,128)}, f32[128,32]{0,1:T(8,128)S(1)}, u32[]{:S(2)}) copy-start(f32[128,32]{0,1:T(8,128)S(1)} %get-tuple-element.53) | copy-start | bytes 49156
  38.1 33.5 %copy-start.17 = (f32[128,512]{1,0:T(8,128)}, f32[128,512]{1,0:T(8,128)S(1)}, u32[]{:S(2)}) copy-start(f32[128,512]{1,0:T(8,128)S(1)} %fusion.41) | copy-start | bytes 786436
  49.1 27.4 %copy-start.20 = (bf16[128,512]{0,1:T(8,128)(2,1)}, bf16[128,512]{0,1:T(8,128)(2,1)S(1)}, u32[]{:S(2)}) copy-start(bf16[128,512]{0,1:T(8,128)(2,1)S(1)} %copy.81) | copy-start | bytes 393220
  49.1 24.7 %copy-start.51 = (f32[128,8]{0,1:T(8,128)}, f32[128,8]{0,1:T(8,128)S(1)}, u32[]{:S(2)}) copy-start(f32[128,8]{0,1:T(8,128)S(1)} %add_rsqrt_fusion.1) | copy-start | bytes 12292
  74.2 2.6 copy-start.28
  74.2 2.6 copy-start.29
  74.2 2.2 copy-start.33
  75.4 22.3 %copy-start.45 = (f32[8,2,128]{2,1,0:T(2,128)}, f32[8,2,128]{2,1,0:T(2,128)S(1)}, u32[]{:S(2)}) copy-start(f32[8,2,128]{2,1,0:T(2,128)S(1)} %log.8) | copy-start | bytes 24580
  76.5 21.3 %copy-start.49 = (f32[4,1,256]{2,1,0:T(1,128)S(1)}, f32[4,1,256]{2,1,0:T(1,128)}, u32[]{:S(2)}) copy-start(f32[4,1,256]{2,1,0:T(1,128)} %convert_element_type.273) | copy-start | bytes 12292
  76.8 90.9 %copy-start.18 = (bf16[8,64,2,128]{3,1,2,0:T(8,128)(2,1)}, bf16[8,64,2,128]{3,1,2,0:T(8,128)(2,1)S(1)}, u32[]{:S(2)}) copy-start(bf16[8,64,2,128]{3,1,2,0:T(8,128)(2,1)S(1)} %convolution_convert_fusion.8) | copy-start | bytes 786436
  97.7 70.0 %copy-start.58 = (f32[128]{0:T(128)}, f32[128]{0:T(128)S(1)}, u32[]{:S(2)}) copy-start(f32[128]{0:T(128)S(1)} %add_rsqrt_fusion.2) | copy-start | bytes 1540
  301.5 7.7 copy-start.8
  301.5 7.7 copy-start.7
  301.5 7.7 copy-start
  301.5 7.7 copy-start.50
  301.5 7.7 copy-start.59
  309.2 3.8 copy-start.25
  309.2 3.7 copy-start.60
  309.2 4.7 copy-start.2
  317.5 1.8 copy-start.42
  317.5 1.8 copy-start.44
  325.8 3.0 copy-start.37
  325.8 3.0 copy-start.53
  331.0 59.3 %reduce-scatter.10.cloned.1.call-start = ((), (), s32[]{:S(2)}) async-start(), calls=%async_computation.15 | async-start | bytes 1310720 | tf_op jit(solution)/shard_map/reduce_scatter | solution.py:254
  341.2 8.4 copy-start.14
  341.2 8.4 copy-start.35
  349.6 68.5 %reduce-scatter.12.cloned.1.call-start = ((), (), s32[]{:S(2)}) async-start(), calls=%async_computation.16 | async-start | bytes 1310720 | tf_op jit(solution)/shard_map/reduce_scatter | solution.py:257
  350.7 2.9 copy-start.6
  350.7 2.9 copy-start.19
  353.5 98.9 %reduce-scatter.14.cloned.1.call-start = ((), (), s32[]{:S(2)}) async-start(), calls=%async_computation.17 | async-start | bytes 2621440 | tf_op jit(solution)/shard_map/reduce_scatter | solution.py:260
  355.6 177.2 %reduce-scatter.16.cloned.1.call-start = ((), (), s32[]{:S(2)}) async-start(), calls=%async_computation.18 | async-start | bytes 11796480 | tf_op jit(solution)/shard_map/reduce_scatter | solution.py:181
  362.1 251.3 %reduce-scatter.18.cloned.1.call-start = ((), (), s32[]{:S(2)}) async-start(), calls=%async_computation.19 | async-start | bytes 11796480 | tf_op jit(solution)/shard_map/reduce_scatter | solution.py:184
  368.5 325.3 %reduce-scatter.20.cloned.1.call-start = ((), (), s32[]{:S(2)}) async-start(), calls=%async_computation.20 | async-start | bytes 11796480 | tf_op jit(solution)/shard_map/reduce_scatter | solution.py:167
  374.7 394.2 %all-gather.26.cloned.1.call-start = ((), (), s32[]{:S(2)}) async-start(), calls=%async_computation.21 | async-start | bytes 4718592 | tf_op jit(solution)/shard_map/all_gather | solution.py:274
  375.3 660.3 %all-reduce.12.cloned.1.call-start = ((), (), s32[]{:S(2)}) async-start(), calls=%async_computation.22 | async-start | bytes 16252928 | tf_op jit(solution)/shard_map/psum | solution.py:279
  693.8 4.1 copy-start.22
  695.4 4.3 copy-start.11
  695.4 4.3 copy-start.24
  695.4 4.3 copy-start.38
  695.4 4.3 copy-start.54
  698.0 2.3 copy-start.57
  1035.6 4.6 copy-start.13
  1040.1 2.7 copy-start.12
  1042.9 2.7 copy-start.27
  1042.9 3.8 copy-start.40
  1045.6 2.0 copy-start.39
  (24 other events, 27.0 us)
Sparse Core Ops, SparseCore 0:
  9.5 19.4 all-gather.13
  30.6 16.6 all-gather.11
  48.9 22.5 all-gather.15
  73.0 22.5 all-gather.17
  97.0 64.2 all-gather.19
  162.6 64.2 all-gather.21
  228.4 64.2 all-gather.23
  331.2 31.1 reduce-scatter.7
  365.5 24.8 reduce-scatter.9
  393.3 24.7 reduce-scatter.11
  421.2 31.1 reduce-scatter.13
  454.8 77.9 reduce-scatter.15
  535.4 77.9 reduce-scatter.17
  615.8 77.9 reduce-scatter.19
  695.8 73.0 all-gather.25
  774.0 261.5 all-reduce.11
